TPU v7x, 32 devices: a whole 2x2x4 slice. The times are simulated.
32 devices in a mesh: dp: 8 (over y, x, core), tensor: 4 (over z).
Axes of the slice: x: 2, y: 2, z: 4, core: 2. Of those that a mesh axis runs over, the one named last changes fastest.
Arguments:
- inputs: bfloat16 [16384, 768], P('dp'), may hold values from -6 to 6
- w_qkv: bfloat16 [768, 3, 768], P(None, None, 'tensor'), may hold values from -0.3125 to 0.3125
- b_qv: float32 [2, 768], P(None, 'tensor'), may hold values from -3 to 3
- w_out: bfloat16 [768, 768], P('tensor'), may hold values from -1.25 to 1.25
- b_out: float32 [768], replicated, may hold values from -3 to 3
- g_one: float32 [768], replicated, may hold values from 0.5 to 1.5
- s_one: float32 [768], replicated, may hold values from -3 to 3
- w_up: bfloat16 [768, 3072], P(None, 'tensor'), may hold values from -0.21875 to 0.21875
- b_up: float32 [3072], P('tensor'), may hold values from -3 to 3
- w_down: bfloat16 [3072, 768], P('tensor'), may hold values from -0.15625 to 0.15625
- b_down: float32 [768], replicated, may hold values from -3 to 3
- g_two: float32 [768], replicated, may hold values from 0.5 to 1.5
- s_two: float32 [768], replicated, may hold values from -3 to 3
- cotangent: bfloat16 [16384, 768], P('dp'), may hold values from -6 to 6
- pad_mask: int32 [16384], P('dp'), may hold values 0 or 1
- doc_lengths: int32 [32], P('dp'), may hold values from 30 to 512, as said below
Outputs:
- out: bfloat16 [16384, 768], P('dp')
- d_inputs: float32 [16384, 768], P('dp')
- d_w_qkv: float32 [768, 3, 768], P(None, None, 'tensor')
- d_b_qv: float32 [2, 768], P(None, 'tensor')
- d_w_out: float32 [768, 768], P('tensor')
- d_b_out: float32 [768], replicated
- d_g_one: float32 [768], replicated
- d_s_one: float32 [768], replicated
- d_w_up: float32 [768, 3072], P(None, 'tensor')
- d_b_up: float32 [3072], P('tensor')
- d_w_down: float32 [3072, 768], P('tensor')
- d_b_down: float32 [768], replicated
- d_g_two: float32 [768], replicated
- d_s_two: float32 [768], replicated
Inputs may be any that keep to these rules, and one draw needn't show every extreme that they name: `doc_lengths`: in every draw one document has 512 true tokens and one has 30. Rows at or beyond a document's count are padding: they are no keys whatever pad_mask says, and their outputs are zero. The first token of a document is always a key.
All inputs are finite; a program needn't handle non-finite values. No bound on the sum of `pad_mask` on one device may be relied on, other than what follows from the above.
Results may differ from a plain program's by a relative error of at most 0.014.
The roundings to bfloat16 on the way count: a program that leaves them out, or rounds other values in their place, can miss the bound.
Values may be sent and summed in bfloat16 or wider, within the bound.
No kernel may reach another device: no remote copies, remote signals or barrier semaphores. Data moves between devices by JAX's collectives and lax.ppermute only.
A program may use at most 128 MiB of HBM per device.

v0:
```python
import jax
import jax.numpy as jnp
from jax import lax
from jax.sharding import PartitionSpec as P

HD = 64


def norm_layer(values, gain, shift):
    center = values - jnp.mean(values, axis=-1, keepdims=True)
    spread = jnp.mean(center * center, axis=-1, keepdims=True)
    return center * lax.rsqrt(spread + 1e-05) * gain + shift


def gelu_exact(values):
    return jax.nn.gelu(values, approximate=False)


def masked_scores(queries, key_rows, key_valid):
    scores = jnp.einsum("qhe,khe->hqk", queries, key_rows, preferred_element_type=jnp.float32)
    return jnp.where(key_valid[None, None, :], scores, -1e30)


def doc_forward(packed):
    queries, key_rows, values, key_valid = packed
    scores = masked_scores(queries, key_rows, key_valid)
    log_total = jax.nn.logsumexp(scores, axis=-1, keepdims=True)
    weights = jnp.exp(scores - log_total).astype(jnp.bfloat16)
    context = jnp.einsum("hqk,khe->qhe", weights, values, preferred_element_type=jnp.float32)
    return (context.astype(jnp.bfloat16), log_total)


def doc_backward(packed):
    queries, key_rows, values, key_valid, log_total, d_context = packed
    scores = masked_scores(queries, key_rows, key_valid)
    weights = jnp.exp(scores - log_total)
    d_prob = jnp.einsum("qhe,khe->hqk", d_context, values, preferred_element_type=jnp.float32)
    d_values = jnp.einsum(
        "hqk,qhe->khe", weights.astype(jnp.bfloat16), d_context, preferred_element_type=jnp.float32
    )
    d_scores = (weights * (d_prob - jnp.sum(d_prob * weights, axis=-1, keepdims=True))).astype(
        jnp.bfloat16
    )
    d_query = jnp.einsum("hqk,khe->qhe", d_scores, key_rows, preferred_element_type=jnp.float32)
    d_keys = jnp.einsum("hqk,qhe->khe", d_scores, queries, preferred_element_type=jnp.float32)
    return (
        d_query.astype(jnp.bfloat16),
        d_keys.astype(jnp.bfloat16),
        d_values.astype(jnp.bfloat16),
    )


def per_device(
    inputs,
    w_qkv,
    b_qv,
    w_out,
    b_out,
    g_one,
    s_one,
    w_up,
    b_up,
    w_down,
    b_down,
    g_two,
    s_two,
    cotangent,
    pad_mask,
    doc_lengths,
):
    rows = inputs.shape[0]
    doc_count = doc_lengths.shape[0]
    length = rows // doc_count
    local_heads = w_qkv.shape[2] // HD
    scale = HD ** (-0.5)
    position = jnp.arange(length, dtype=jnp.int32)
    inside = position[None, :] < doc_lengths[:, None]
    key_valid = inside & ((pad_mask.reshape(doc_count, length) == 1) | (position[None, :] == 0))
    row_weight = inside.astype(jnp.float32).reshape(rows, 1)
    projected = jnp.einsum("td,dce->tce", inputs, w_qkv, preferred_element_type=jnp.float32)
    queries = ((projected[:, 0] + b_qv[0]) * scale).astype(jnp.bfloat16)
    key_rows = projected[:, 1].astype(jnp.bfloat16)
    values = (projected[:, 2] + b_qv[1]).astype(jnp.bfloat16)
    shaped = (doc_count, length, local_heads, HD)
    queries_doc = queries.reshape(shaped)
    keys_doc = key_rows.reshape(shaped)
    values_doc = values.reshape(shaped)
    context, log_total = lax.map(doc_forward, (queries_doc, keys_doc, values_doc, key_valid))
    context = context.reshape(rows, local_heads * HD)
    heads_part = jnp.dot(context, w_out, preferred_element_type=jnp.float32)
    attn = lax.psum(heads_part, "tensor")
    z_one = inputs.astype(jnp.float32) + attn + b_out
    h_one, pull_one = jax.vjp(norm_layer, z_one, g_one, s_one)
    h_low = h_one.astype(jnp.bfloat16)
    up_value = jnp.dot(h_low, w_up, preferred_element_type=jnp.float32) + b_up
    act, pull_act = jax.vjp(gelu_exact, up_value)
    act_low = act.astype(jnp.bfloat16)
    down_part = jnp.dot(act_low, w_down, preferred_element_type=jnp.float32)
    down = lax.psum(down_part, "tensor")
    z_two = h_one + down + b_down
    normed, pull_two = jax.vjp(norm_layer, z_two, g_two, s_two)
    d_ztwo, d_gtwo, d_stwo = pull_two(cotangent.astype(jnp.float32) * row_weight)
    d_bdown = jnp.sum(d_ztwo, axis=0)
    result = (normed * row_weight).astype(jnp.bfloat16)
    dz_two_low = d_ztwo.astype(jnp.bfloat16)
    d_wdown = jnp.einsum("tf,td->fd", act_low, dz_two_low, preferred_element_type=jnp.float32)
    d_act = jnp.einsum("td,fd->tf", dz_two_low, w_down, preferred_element_type=jnp.float32)
    d_up_low = pull_act(d_act)[0].astype(jnp.bfloat16)
    d_bup = jnp.sum(d_up_low, axis=0, dtype=jnp.float32)
    d_wup = jnp.einsum("td,tf->df", h_low, d_up_low, preferred_element_type=jnp.float32)
    hone_part = jnp.einsum("tf,df->td", d_up_low, w_up, preferred_element_type=jnp.float32)
    d_hone = lax.psum(hone_part, "tensor") + d_ztwo
    d_zone, d_gone, d_sone = pull_one(d_hone)
    d_bout = jnp.sum(d_zone, axis=0)
    dz_one_low = d_zone.astype(jnp.bfloat16)
    d_wout = jnp.einsum("th,td->hd", context, dz_one_low, preferred_element_type=jnp.float32)
    d_context = jnp.einsum(
        "td,hd->th", dz_one_low, w_out, preferred_element_type=jnp.float32
    ).astype(jnp.bfloat16)
    back_items = (
        queries_doc,
        keys_doc,
        values_doc,
        key_valid,
        log_total,
        d_context.reshape(shaped),
    )
    d_query, d_keys, d_values = lax.map(doc_backward, back_items)
    d_query = d_query.reshape(rows, local_heads * HD) * jnp.asarray(scale, jnp.bfloat16)
    stacked = jnp.stack(
        [d_query, d_keys.reshape(rows, local_heads * HD), d_values.reshape(rows, local_heads * HD)],
        axis=1,
    )
    d_wqkv = jnp.einsum("td,tce->dce", inputs, stacked, preferred_element_type=jnp.float32)
    d_bqv = jnp.stack(
        [
            jnp.sum(stacked[:, 0], axis=0, dtype=jnp.float32),
            jnp.sum(stacked[:, 2], axis=0, dtype=jnp.float32),
        ]
    )
    input_part = jnp.einsum("tce,dce->td", stacked, w_qkv, preferred_element_type=jnp.float32)
    d_inputs = lax.psum(input_part, "tensor") + d_zone
    summed = lax.psum(
        (
            d_wqkv,
            d_bqv,
            d_wout,
            d_bout,
            d_gone,
            d_sone,
            d_wup,
            d_bup,
            d_wdown,
            d_bdown,
            d_gtwo,
            d_stwo,
        ),
        "dp",
    )
    return (
        result,
        d_inputs,
        summed[0],
        summed[1],
        summed[2],
        summed[3],
        summed[4],
        summed[5],
        summed[6],
        summed[7],
        summed[8],
        summed[9],
        summed[10],
        summed[11],
    )


def solution(mesh):
    placed = (
        P("dp", None),
        P(None, None, "tensor"),
        P(None, "tensor"),
        P("tensor", None),
        P(),
        P(),
        P(),
        P(None, "tensor"),
        P("tensor"),
        P("tensor", None),
        P(),
        P(),
        P(),
        P("dp", None),
        P("dp"),
        P("dp"),
    )
    return jax.shard_map(
        per_device,
        mesh=mesh,
        in_specs=placed,
        out_specs=(
            P("dp", None),
            P("dp", None),
            P(None, None, "tensor"),
            P(None, "tensor"),
            P("tensor", None),
            P(),
            P(),
            P(),
            P(None, "tensor"),
            P("tensor"),
            P("tensor", None),
            P(),
            P(),
            P(),
        ),
        check_vma=False,
    )
```

profile of v0, /device:TPU:0, one launch (start us, length us, event | category | flops | bytes accessed | tf_op | source)
XLA Modules:
  0.0 1201.6 jit_solution(13847251560515117021)
XLA Ops:
  7.2 4.2 fusion.90
  11.5 1.3 fusion.89
  13.5 3.1 squeeze.34
  16.6 2.2 squeeze.35
  21.1 2.9 fusion.73
  25.0 13.6 %while.26 = (s32[]{:T(128)}, bf16[4,512,3,64]{1,3,2,0:T(8,128)(2,1)}, f32[4,3,512,1]{2,1,3,0:T(4,128)}, bf16[4,512,3,64]{1,3,2,0:T(8,128)(2,1)S(1)}, pred[4,512]...) while((s32[]{:T(128)}, ...), condition=%wide.region_3.4_spmd, body=%wide.region_0.3_spmd.sunk | while | flops 207728640 | bytes 10306649 | solution.py:88
  26.9 1.5 fusion.134
  30.3 1.5 fusion.134
  33.7 1.5 fusion.134
  37.1 1.5 fusion.134
  38.6 2.0 copy.49
  41.7 4.7 fusion.91
  46.9 225.2 %all-reduce.8.cloned.1.call-done = f32[2048,768]{1,0:T(8,128)} async-done(((f32[2048,768]{1,0:T(8,128)}), f32[2048,768]{1,0:T(8,128)}) %all-reduce.8.cloned.1.call-update) | async-done | bytes 6291472 | tf_op jit(solution)/shard_map/psum | solution.py:91
  272.2 4.6 fusion.88
  277.7 1.1 fusion.69
  279.4 18.3 %multiply_convert_fusion.2 = (bf16[2048,768]{1,0:T(8,128)(2,1)S(1)}, f32[2048,768]{1,0:T(8,128)}, f32[2048,768]{1,0:T(8,128)}) fusion(f32[768]{0:T(1024)S(1)} %copy-done.35, bf16[2048,768]{1,0:T(8,128)(2,1)S(1)} %fusion.69, bf16[768,768]{1,0:T(8,128)(2,1)S(1)} %copy-done), kind=kOutput, calls=%fused_computation.84 | convolution fusion | flops 2519728128 | bytes 20057088 | tf_op jit(solution)/shard_map/dot_general | solution.py:95
  297.8 1.8 copy-done.37
  299.5 4.5 fusion.92
  304.2 221.7 %all-reduce.10.cloned.1.call-done = f32[2048,768]{1,0:T(8,128)} async-done(((f32[2048,768]{1,0:T(8,128)}), f32[2048,768]{1,0:T(8,128)}) %all-reduce.10.cloned.1.call-update) | async-done | bytes 6291472 | tf_op jit(solution)/shard_map/psum | solution.py:99
  525.9 5.7 fusion.86
  532.5 1.0 copy-done.5
  533.5 3.6 multiply_reduce_fusion.1
  537.2 4.9 fusion.85
  542.1 9.3 convert_reduce_fusion
  551.4 1.7 copy-done.36
  553.1 4.5 fusion.93
  557.9 221.6 %all-reduce.12.cloned.1.call-done = f32[2048,768]{1,0:T(8,128)} async-done(((f32[2048,768]{1,0:T(8,128)}), f32[2048,768]{1,0:T(8,128)}) %all-reduce.12.cloned.1.call-update) | async-done | bytes 6291472 | tf_op jit(solution)/shard_map/psum | solution.py:112
  779.5 8.7 multiply_reduce_fusion.2
  788.3 4.3 fusion.84
  792.6 2.7 copy-done.3
  795.3 1.3 convolution_convert_fusion.2
  797.2 1.0 copy.51
  799.3 30.5 %while.27 = (s32[]{:T(128)}, bf16[4,512,3,64]{1,3,2,0:T(8,128)(2,1)S(1)}, bf16[4,512,3,64]{1,3,2,0:T(8,128)(2,1)}, bf16[4,512,3,64]{1,3,2,0:T(8,128)(2,1)S(1)}, ...) while((s32[]{:T(128)}, ...), condition=%wide.region_17.18_spmd, body=%wide.region_15.17_spmd.sunk | while | flops 513047040 | bytes 25611892 | solution.py:128
  800.7 2.0 multiply_reduce_fusion.8
  803.5 1.3 fusion.146
  805.2 1.7 fusion.147
  808.3 2.0 multiply_reduce_fusion.8
  811.2 1.3 fusion.146
  812.8 1.7 fusion.147
  816.0 2.0 multiply_reduce_fusion.8
  818.8 1.3 fusion.146
  820.5 1.7 fusion.147
  823.6 2.0 multiply_reduce_fusion.8
  826.4 1.3 fusion.146
  828.1 1.7 fusion.147
  830.6 1.5 mul.219
  832.0 2.1 constant_dynamic-update-slice_fusion.2
  835.3 1.5 copy.54
  836.8 2.3 stack_reshape.7
  839.2 1.0 constant_dynamic-update-slice_fusion.1
  840.1 1.0 constant_dynamic-update-slice_fusion
  841.1 7.2 convolution_bitcast_fusion
  848.3 7.1 fusion.94
  855.4 7.1 fusion.81
  862.6 1.8 fusion.83
  865.4 3.2 fusion.75
  870.1 200.1 %all-reduce.14.cloned.1.call-done = f32[2048,768]{1,0:T(8,128)} async-done(((f32[2048,768]{1,0:T(8,128)}), f32[2048,768]{1,0:T(8,128)}) %all-reduce.14.cloned.1.call-update) | async-done | bytes 6291472 | tf_op jit(solution)/shard_map/psum | solution.py:142
  1070.1 7.7 add_reduce_fusion
  1077.8 26.2 %all-reduce = (f32[2,192]{1,0:T(2,128)}, f32[768]{0:T(1024)}, f32[768]{0:T(1024)}, f32[768]{0:T(1024)}, f32[768]{0:T(1024)}, /*index=5*/f32[768]{0:T(1024)}, f32[768]{0:T(1024)}, f32[768]{0:T(1024)}) all-reduce(f32[2,192]{1,0:T(2,128)S(1)} %pad_maximum_fusion, ...), channel_id=1, replica_groups=mesh['dp'=8,'tensor'=4] {'dp'}, use_global_device_ids=true, to_apply=%region_22.23 | all-reduce | flops 5760 | bytes 46080 | tf_op jit(solution)/shard_map/psum | solution.py:143
  1104.1 82.9 %all-reduce.16.cloned.1.call-done = (f32[768,3,192]{0,2,1:T(8,128)}, f32[192,768]{1,0:T(8,128)}, f32[768,768]{1,0:T(8,128)}, f32[768,768]{1,0:T(8,128)}) async-done(((f32[768,3,192]{0,2,1:T(8,128)}, f32[192,768]{1,0:T(8,128)}, f32[768,768]{1,0:T(8,128)}, f32[768,768]{1,0:T(8,128)}), (f32[768,3,192]{0,2,1:T(8,128)}, f32[192,768]{1,0:T(8,128)}, f32[768,768]{1,0:T(8,128)}, ...) | async-done | bytes 7077904 | tf_op jit(solution)/shard_map/psum | solution.py:143
  1187.0 2.9 copy.107
  1189.9 1.9 copy.108
  1191.8 1.4 copy.109
  1193.2 1.4 copy.110
  (175 shorter events, 32.2 us)
Async XLA Ops:
  7.2 272.2 %copy-start = (bf16[768,768]{1,0:T(8,128)(2,1)S(1)}, bf16[768,768]{1,0:T(8,128)(2,1)}, u32[]{:S(2)}) copy-start(bf16[768,768]{1,0:T(8,128)(2,1)} %param.27) | copy-start | bytes 3538948
  7.2 265.0 %all-reduce.8.cloned.1.call-start = ((), (), s32[]{:S(2)}) async-start(), calls=%async_computation | async-start | bytes 12582912 | tf_op jit(solution)/shard_map/psum | solution.py:91
  11.5 7.3 copy-start.32
  12.8 7.5 copy-start.27
  38.6 7.8 copy-start.10
  40.8 0.9 copy-start.6
  41.7 230.5 %copy-start.29 = (f32[768]{0:T(1024)S(1)}, f32[768]{0:T(1024)}, u32[]{:S(2)}) copy-start(f32[768]{0:T(1024)} %param.24) | copy-start | bytes 9220
  46.4 479.5 %all-reduce.10.cloned.1.call-start = ((), (), s32[]{:S(2)}) async-start(), calls=%async_computation.1 | async-start | bytes 12582912 | tf_op jit(solution)/shard_map/psum | solution.py:99
  276.8 2.7 copy-start.2
  276.8 0.9 copy-start.18
  276.8 0.9 copy-start.23
  277.7 1.8 copy-start.35
  279.4 18.3 %copy-start.12 = (bf16[2048,768]{1,0:T(8,128)(2,1)}, bf16[2048,768]{1,0:T(8,128)(2,1)S(1)}, u32[]{:S(2)}) copy-start(bf16[2048,768]{1,0:T(8,128)(2,1)S(1)} %fusion.69) | copy-start | bytes 9437188
  279.4 20.1 %copy-start.33 = (bf16[768,768]{1,0:T(8,128)(2,1)S(1)}, bf16[768,768]{1,0:T(8,128)(2,1)}, u32[]{:S(2)}) copy-start(bf16[768,768]{1,0:T(8,128)(2,1)} %param.29) | copy-start | bytes 3538948
  297.8 1.8 copy-start.37
  304.0 221.9 %copy-start.30 = (f32[768]{0:T(1024)S(1)}, f32[768]{0:T(1024)}, u32[]{:S(2)}) copy-start(f32[768]{0:T(1024)} %param.30) | copy-start | bytes 9220
  304.0 475.5 %all-reduce.12.cloned.1.call-start = ((), (), s32[]{:S(2)}) async-start(), calls=%async_computation.2 | async-start | bytes 12582912 | tf_op jit(solution)/shard_map/psum | solution.py:112
  531.6 1.9 copy-start.5
  531.6 1.9 copy-start.22
  532.5 4.6 copy-start.31
  533.5 8.5 slice-start.2
  537.1 4.9 copy-start.34
  537.1 4.9 slice-start.3
  542.0 9.4 copy-start.4
  542.0 237.5 %copy-start.19 = (f32[2048]{0:T(1024)}, f32[2048]{0:T(1024)S(1)}, u32[]{:S(2)}) copy-start(f32[2048]{0:T(1024)S(1)} %negate_multiply_fusion.2) | copy-start | bytes 24580
  551.4 1.7 copy-start.36
  557.6 512.5 %all-reduce.14.cloned.1.call-start = ((), (), s32[]{:S(2)}) async-start(), calls=%async_computation.3 | async-start | bytes 12582912 | tf_op jit(solution)/shard_map/psum | solution.py:142
  788.3 7.0 copy-start.16
  792.6 2.7 copy-start.3
  829.8 9.3 copy-start.8
  829.9 4.3 copy-start.11
  848.2 7.1 copy-start.20
  848.3 338.7 %all-reduce.16.cloned.1.call-start = ((), (), s32[]{:S(2)}) async-start(), calls=%async_computation.4 | async-start | bytes 14155776 | tf_op jit(solution)/shard_map/psum | solution.py:143
  848.3 7.1 copy-start.38
  848.3 14.2 %slice-start = ((s8[6291456]{0:T(1024)(128)(4,1)}), s8[4194304]{0:T(1024)(128)(4,1)S(1)}, s32[]{:S(2)}) async-start(s8[6291456]{0:T(1024)(128)(4,1)} %bitcast.157), calls=%async_computation.5 | async-start | bytes 8388608
  855.4 7.1 slice-start.1
  855.4 7.1 copy-start.7
  862.5 1.9 copy-start.13
  862.5 2.8 copy-start.17
  868.6 1.1 copy-start.9
  870.0 207.8 %copy-start.21 = (f32[768]{0:T(1024)S(1)}, f32[768]{0:T(1024)}, u32[]{:S(2)}) copy-start(f32[768]{0:T(1024)} %get-tuple-element.150) | copy-start | bytes 9220
  870.0 207.8 %copy-start.24 = (f32[768]{0:T(1024)S(1)}, f32[768]{0:T(1024)}, u32[]{:S(2)}) copy-start(f32[768]{0:T(1024)} %get-tuple-element.145) | copy-start | bytes 9220
  870.1 207.8 %copy-start.25 = (f32[768]{0:T(1024)S(1)}, f32[768]{0:T(1024)}, u32[]{:S(2)}) copy-start(f32[768]{0:T(1024)} %get-tuple-element.149) | copy-start | bytes 9220
  870.1 207.7 %copy-start.26 = (f32[768]{0:T(1024)S(1)}, f32[768]{0:T(1024)}, u32[]{:S(2)}) copy-start(f32[768]{0:T(1024)} %get-tuple-element.215) | copy-start | bytes 9220
  870.1 207.7 %copy-start.28 = (f32[768]{0:T(1024)S(1)}, f32[768]{0:T(1024)}, u32[]{:S(2)}) copy-start(f32[768]{0:T(1024)} %get-tuple-element.223) | copy-start | bytes 9220
  1187.0 4.9 copy-start.15
  1187.0 6.3 copy-start.14
  1187.0 7.7 copy-start.1
Sparse Core Ops, SparseCore 0:
  46.5 225.5 all-reduce.7
  304.1 221.7 all-reduce.9
  557.8 221.7 all-reduce.11
  848.4 221.7 all-reduce.13
  1074.8 112.0 all-reduce.15
where the time goes:
time: 1210 us; the launch traced here: 1200 us
  waiting for transfers between devices  952 us (79%)
  matrix products  106 us (9%)
  other arithmetic  55.1 us (5%)
  local copies, waits for them, and re-layouts  46.6 us (4%)
  blocking collectives  26.2 us (2%)
  between operations  14.8 us (1%)
    psum x1, waiting for transfers between devices, per_device(): attn = lax.psum(heads_part, 'tensor')  225 us
    psum x1, waiting for transfers between devices, per_device(): down = lax.psum(down_part, 'tensor')  222 us
    psum x1, waiting for transfers between devices, per_device(): d_hone = lax.psum(hone_part, 'tensor') + d_ztwo  222 us
    psum x1, waiting for transfers between devices, per_device(): d_inputs = lax.psum(input_part, 'tensor') + d_zone  200 us
    psum x1, waiting for transfers between devices, per_device(): lax.psum((d_wqkv, d_bqv, d_wout, d_bout, d_gone, d_sone, d_wup, d_bup, d_...  82.9 us
    psum x1, blocking collectives, per_device(): lax.psum((d_wqkv, d_bqv, d_wout, d_bout, d_gone, d_sone, d_wup, d_bup, d_...  26.2 us
  transfers between devices with their start and end apart: 5, of which 5 were waited for; matrix products, arithmetic and copies ran while one was open for 2% of the time, Pallas kernels for 0%

commit v1 on v0

--- a/solution.py
+++ b/solution.py
@@ -4,6 +4,14 @@
 from jax.sharding import PartitionSpec as P
 
 HD = 64
+
+
+def doubling_sum(x, mesh_axis):
+    size, total = (lax.axis_size(mesh_axis), x)
+    for far in [1 << k for k in range(size.bit_length() - 1)]:
+        pairs = [(i, i ^ far) for i in range(size)]
+        total = total + lax.ppermute(total, mesh_axis, pairs)
+    return total
 
 
 def norm_layer(values, gain, shift):
@@ -88,7 +96,7 @@
     context, log_total = lax.map(doc_forward, (queries_doc, keys_doc, values_doc, key_valid))
     context = context.reshape(rows, local_heads * HD)
     heads_part = jnp.dot(context, w_out, preferred_element_type=jnp.float32)
-    attn = lax.psum(heads_part, "tensor")
+    attn = doubling_sum(heads_part, "tensor")
     z_one = inputs.astype(jnp.float32) + attn + b_out
     h_one, pull_one = jax.vjp(norm_layer, z_one, g_one, s_one)
     h_low = h_one.astype(jnp.bfloat16)

time: 1210 us -> 1400 us (1.16)
  waiting for transfers between devices: 952 us -> 1110 us
  local copies, waits for them, and re-layouts: 46.6 us -> 66.8 us
    ppermute x0 -> x2, waiting for transfers between devices: none -> 401 us  [doubling_sum(): total = total + lax.ppermute(total, mesh_axis, pairs)]
    psum x1 -> x0, waiting for transfers between devices: 225 us -> none  [per_device(): attn = lax.psum(heads_part, 'tensor')]
    unnamed x94 -> x88, local copies, waits for them, and re-layouts: 21.4 us -> 41.7 us
  transfers between devices with their start and end apart: 5 -> 6, of which waited for: 5 -> 6; matrix products, arithmetic and copies ran while one was open for 2% -> 4% of each run, Pallas kernels for 0% -> 0%
where the time goes in v1:
time: 1400 us; the launch traced here: 1390 us
  waiting for transfers between devices  1110 us (79%)
  matrix products  104 us (7%)
  local copies, waits for them, and re-layouts  66.8 us (5%)
  other arithmetic  61.7 us (4%)
  blocking collectives  25.9 us (2%)
  between operations  14.7 us (1%)
    ppermute x2, waiting for transfers between devices, doubling_sum(): total = total + lax.ppermute(total, mesh_axis, pairs)  401 us
    psum x1, waiting for transfers between devices, per_device(): d_hone = lax.psum(hone_part, 'tensor') + d_ztwo  222 us
    psum x1, waiting for transfers between devices, per_device(): down = lax.psum(down_part, 'tensor')  219 us
    psum x1, waiting for transfers between devices, per_device(): d_inputs = lax.psum(input_part, 'tensor') + d_zone  196 us
    psum x1, waiting for transfers between devices, per_device(): lax.psum((d_wqkv, d_bqv, d_wout, d_bout, d_gone, d_sone, d_wup, d_bup, d_...  76.1 us
    unnamed x88, local copies, waits for them, and re-layouts  41.7 us
  transfers between devices with their start and end apart: 6, of which 6 were waited for; matrix products, arithmetic and copies ran while one was open for 4% of the time, Pallas kernels for 0%

profile of v1, /device:TPU:0, one launch (start us, length us, event | category | flops | bytes accessed | tf_op | source)
XLA Modules:
  0.0 1393.2 jit_solution(12779254341649545562)
XLA Ops:
  7.2 4.2 fusion.90
  11.5 1.4 fusion.89
  13.5 3.1 squeeze.34
  16.6 2.2 squeeze.35
  21.1 2.9 fusion.73
  25.0 13.6 while.26
  26.9 1.5 fusion.134
  30.3 1.5 fusion.134
  33.7 1.5 fusion.134
  37.1 1.5 fusion.134
  38.6 2.0 copy.57
  40.8 2.2 fusion.91
  43.0 3.1 collective-permute-start
  46.1 135.5 %collective-permute-done = f32[2048,768]{0,1:T(8,128)S(1)} collective-permute-done((f32[2048,768]{0,1:T(8,128)S(1)}, f32[2048,768]{0,1:T(8,128)S(1)}, u32[]{:S(2)}, u32[]{:S(2)}) %collective-permute-start) | collective-permute-done | bytes 6291488 | tf_op jit(solution)/shard_map/ppermute | solution.py:13
  181.6 4.0 add.159
  185.6 2.8 collective-permute-start.1
  188.4 4.8 copy.53
  193.2 265.1 %collective-permute-done.1 = f32[2048,768]{0,1:T(8,128)} collective-permute-done((f32[2048,768]{0,1:T(8,128)}, f32[2048,768]{0,1:T(8,128)}, u32[]{:S(2)}, u32[]{:S(2)}) %collective-permute-start.1) | collective-permute-done | bytes 6291488 | tf_op jit(solution)/shard_map/ppermute | solution.py:13
  458.4 7.5 fusion.88
  468.5 18.6 %multiply_convert_fusion.2 = (bf16[2048,768]{1,0:T(8,128)(2,1)S(1)}, f32[2048,768]{1,0:T(8,128)}, f32[2048,768]{1,0:T(8,128)}) fusion(f32[768]{0:T(1024)S(1)} %copy-done.30, bf16[2048,768]{0,1:T(8,128)(2,1)S(1)} %fusion.69, bf16[768,768]{1,0:T(8,128)(2,1)S(1)} %copy-done), kind=kOutput, calls=%fused_computation.84 | convolution fusion | flops 2519728128 | bytes 20057088 | tf_op jit(solution)/shard_map/dot_general | solution.py:103
  487.1 1.7 copy-done.32
  488.9 4.5 fusion.92
  493.5 5.0 copy.59
  498.5 218.9 %all-reduce.7.cloned.1.call-done = f32[2048,768]{0,1:T(8,128)} async-done(((f32[2048,768]{0,1:T(8,128)}), f32[2048,768]{0,1:T(8,128)}) %all-reduce.7.cloned.1.call-update) | async-done | bytes 6291472 | tf_op jit(solution)/shard_map/psum | solution.py:107
  717.5 5.6 fusion.86
  724.9 3.7 multiply_reduce_fusion.1
  728.7 5.1 fusion.85
  733.9 10.0 convert_reduce_fusion
  743.9 1.7 copy-done.31
  745.6 4.5 fusion.93
  750.1 221.8 %all-reduce.9.cloned.1.call-done = f32[2048,768]{0,1:T(8,128)} async-done(((f32[2048,768]{0,1:T(8,128)}), f32[2048,768]{0,1:T(8,128)}) %all-reduce.9.cloned.1.call-update) | async-done | bytes 6291472 | tf_op jit(solution)/shard_map/psum | solution.py:120
  972.0 8.7 multiply_reduce_fusion.2
  980.7 3.9 fusion.84
  984.6 2.7 copy-done.3
  990.9 30.5 %while.27 = (s32[]{:T(128)}, bf16[4,512,3,64]{1,3,2,0:T(8,128)(2,1)S(1)}, bf16[4,512,3,64]{1,3,2,0:T(8,128)(2,1)}, bf16[4,512,3,64]{1,3,2,0:T(8,128)(2,1)S(1)}, ...) while((s32[]{:T(128)}, ...), condition=%wide.region_16.17_spmd, body=%wide.region_14.16_spmd.sunk | while | flops 513047040 | bytes 25611892 | solution.py:136
  992.3 2.0 multiply_reduce_fusion.8
  995.1 1.3 fusion.146
  996.7 1.7 fusion.147
  999.9 2.0 multiply_reduce_fusion.8
  1004.4 1.7 fusion.147
  1007.5 2.0 multiply_reduce_fusion.8
  1010.3 1.3 fusion.146
  1012.0 1.7 fusion.147
  1015.1 2.0 multiply_reduce_fusion.8
  1019.6 1.7 fusion.147
  1022.1 1.5 mul.219
  1023.6 2.1 constant_dynamic-update-slice_fusion.2
  1026.8 1.5 copy.65
  1028.3 2.3 stack_reshape.7
  1032.5 7.2 convolution_bitcast_fusion
  1039.8 7.0 fusion.94
  1046.8 7.0 fusion.78
  1053.9 2.0 fusion.80
  1056.7 3.2 fusion.75
  1059.9 4.9 copy.67
  1065.4 196.2 %all-reduce.11.cloned.1.call-done = f32[2048,768]{0,1:T(8,128)} async-done(((f32[2048,768]{0,1:T(8,128)}), f32[2048,768]{0,1:T(8,128)}) %all-reduce.11.cloned.1.call-update) | async-done | bytes 6291472 | tf_op jit(solution)/shard_map/psum | solution.py:150
  1261.7 8.0 add_reduce_fusion
  1269.6 7.0 copy.68
  1276.6 25.9 %all-reduce = (f32[2,192]{1,0:T(2,128)}, f32[768]{0:T(1024)}, f32[768]{0:T(1024)}, f32[768]{0:T(1024)}, f32[768]{0:T(1024)}, /*index=5*/f32[768]{0:T(1024)}, f32[768]{0:T(1024)}, f32[768]{0:T(1024)}) all-reduce(f32[2,192]{1,0:T(2,128)S(1)} %pad_maximum_fusion, ...), channel_id=1, replica_groups=mesh['dp'=8,'tensor'=4] {'dp'}, use_global_device_ids=true, to_apply=%region_21.22 | all-reduce | flops 5760 | bytes 46080 | tf_op jit(solution)/shard_map/psum | solution.py:151
  1302.5 76.1 %all-reduce.13.cloned.1.call-done = (f32[768,3,192]{0,2,1:T(8,128)}, f32[192,768]{1,0:T(8,128)}, f32[768,768]{1,0:T(8,128)}, f32[768,768]{1,0:T(8,128)}) async-done(((f32[768,3,192]{0,2,1:T(8,128)}, f32[192,768]{1,0:T(8,128)}, f32[768,768]{1,0:T(8,128)}, f32[768,768]{1,0:T(8,128)}), (f32[768,3,192]{0,2,1:T(8,128)}, f32[192,768]{1,0:T(8,128)}, f32[768,768]{1,0:T(8,128)}, ...) | async-done | bytes 7077904 | tf_op jit(solution)/shard_map/psum | solution.py:151
  1378.6 2.9 copy.124
  1381.5 1.9 copy.125
  1383.4 1.4 copy.126
  1384.8 1.4 copy.127
  (171 shorter events, 37.9 us)
Async XLA Ops:
  7.2 461.3 %copy-start = (bf16[768,768]{1,0:T(8,128)(2,1)S(1)}, bf16[768,768]{1,0:T(8,128)(2,1)}, u32[]{:S(2)}) copy-start(bf16[768,768]{1,0:T(8,128)(2,1)} %param.27) | copy-start | bytes 3538948
  7.2 710.3 %all-reduce.7.cloned.1.call-start = ((), (), s32[]{:S(2)}) async-start(), calls=%async_computation | async-start | bytes 12582912 | tf_op jit(solution)/shard_map/psum | solution.py:107
  11.5 7.3 copy-start.27
  12.8 7.5 copy-start.22
  38.6 4.4 copy-start.10
  40.8 144.9 %copy-start.6 = (bf16[24,8,4,512]{3,1,2,0:T(8,128)(2,1)}, bf16[24,8,4,512]{3,1,2,0:T(8,128)(2,1)S(1)}, u32[]{:S(2)}) copy-start(bf16[24,8,4,512]{3,1,2,0:T(8,128)(2,1)S(1)} %copy.77) | copy-start | bytes 2359300
  43.0 138.6 %collective-permute-start = (f32[2048,768]{0,1:T(8,128)S(1)}, f32[2048,768]{0,1:T(8,128)S(1)}, u32[]{:S(2)}, u32[]{:S(2)}) collective-permute-start(f32[2048,768]{0,1:T(8,128)S(1)} %fusion.91), channel_id=1, source_target_pairs={{0,1},{1,0},{2,3},{3,2},{4,5},{5,4},{6,7},{7,6},{8,9},{9,8},{10,11... | collective-permute-start | bytes 18874376 | tf_op jit(solution)/shard_map/ppermute | solution.py:13
  185.6 272.7 %copy-start.24 = (f32[768]{0:T(1024)S(1)}, f32[768]{0:T(1024)}, u32[]{:S(2)}) copy-start(f32[768]{0:T(1024)} %param.24) | copy-start | bytes 9220
  185.6 272.7 %collective-permute-start.1 = (f32[2048,768]{0,1:T(8,128)}, f32[2048,768]{0,1:T(8,128)}, u32[]{:S(2)}, u32[]{:S(2)}) collective-permute-start(f32[2048,768]{0,1:T(8,128)} %add.159), channel_id=1, source_target_pairs={{0,2},{1,3},{2,0},{3,1},{4,6},{5,7},{6,4},{7,5},{8,10},{9,11},{10,... | collective-permute-start | bytes 18874376 | tf_op jit(solution)/shard_map/ppermute | solution.py:13
  465.8 2.7 copy-start.2
  465.8 0.8 copy-start.18
  465.8 0.8 copy-start.21
  466.6 1.9 copy-start.30
  468.5 18.6 %copy-start.13 = (bf16[2048,768]{0,1:T(8,128)(2,1)}, bf16[2048,768]{0,1:T(8,128)(2,1)S(1)}, u32[]{:S(2)}) copy-start(bf16[2048,768]{0,1:T(8,128)(2,1)S(1)} %fusion.69) | copy-start | bytes 9437188
  468.5 20.4 %copy-start.28 = (bf16[768,768]{1,0:T(8,128)(2,1)S(1)}, bf16[768,768]{1,0:T(8,128)(2,1)}, u32[]{:S(2)}) copy-start(bf16[768,768]{1,0:T(8,128)(2,1)} %param.29) | copy-start | bytes 3538948
  487.1 1.8 copy-start.32
  493.4 224.1 %copy-start.25 = (f32[768]{0:T(1024)S(1)}, f32[768]{0:T(1024)}, u32[]{:S(2)}) copy-start(f32[768]{0:T(1024)} %param.30) | copy-start | bytes 9220
  493.4 478.6 %all-reduce.9.cloned.1.call-start = ((), (), s32[]{:S(2)}) async-start(), calls=%async_computation.1 | async-start | bytes 12582912 | tf_op jit(solution)/shard_map/psum | solution.py:120
  723.0 1.9 copy-start.4
  723.1 1.9 copy-start.20
  723.8 4.9 copy-start.26
  724.9 8.9 slice-start.2
  728.7 5.2 copy-start.29
  728.7 5.2 slice-start.3
  733.9 10.0 copy-start.5
  743.9 1.7 copy-start.31
  750.1 511.6 %all-reduce.11.cloned.1.call-start = ((), (), s32[]{:S(2)}) async-start(), calls=%async_computation.2 | async-start | bytes 12582912 | tf_op jit(solution)/shard_map/psum | solution.py:150
  980.7 6.6 copy-start.16
  984.6 2.7 copy-start.3
  1021.4 9.3 copy-start.8
  1021.4 4.3 copy-start.12
  1039.7 338.8 %all-reduce.13.cloned.1.call-start = ((), (), s32[]{:S(2)}) async-start(), calls=%async_computation.3 | async-start | bytes 14155776 | tf_op jit(solution)/shard_map/psum | solution.py:151
  1039.8 7.0 copy-start.33
  1039.8 14.0 %slice-start = ((s8[6291456]{0:T(1024)(128)(4,1)}), s8[4194304]{0:T(1024)(128)(4,1)S(1)}, s32[]{:S(2)}) async-start(s8[6291456]{0:T(1024)(128)(4,1)} %bitcast.157), calls=%async_computation.4 | async-start | bytes 8388608
  1046.8 7.0 slice-start.1
  1046.8 7.0 copy-start.7
  1053.8 2.0 copy-start.11
  1053.9 2.8 copy-start.17
  1059.9 5.2 copy-start.9
  1269.6 7.0 copy-start.19
  1269.6 7.0 copy-start.23
  1378.5 4.9 copy-start.15
  1378.6 6.3 copy-start.14
  1378.6 7.7 copy-start.1
Sparse Core Ops, SparseCore 0:
  493.5 223.8 all-reduce.6
  750.2 221.7 all-reduce.8
  1039.9 221.7 all-reduce.10
  1266.3 112.1 all-reduce.12
